TPU v7x, 128 devices: a whole 4x4x4 slice. The times are simulated.
128 devices in a mesh: row: 8 (over x_lo, z), col: 16 (over x_hi, y, core).
Axes of the slice: x: 4 (x_hi: 2, x_lo: 2; x = x_hi * 2 + x_lo), y: 4, z: 4, core: 2. Of those that a mesh axis runs over, the one named last changes fastest.
Arguments:
- hessian: float32 [18432, 18432], P('row', 'col'), may hold values from -1 to 5, as said below
- right_side: float32 [18432, 512], P('row'), may hold values from -6 to 6
- mask: int32 [18432, 512], P('row'), may hold values 0 or 1
- damping: float32 [1], replicated, may hold values from 0.4 to 1.2
Outputs:
- solution: float32 [18432, 512], P('row')
Inputs may be any that keep to these rules, and one draw needn't show every extreme that they name: hessian is symmetric and positive definite.
All inputs are finite; a program needn't handle non-finite values. No bound on the sum of `mask` on one device may be relied on, other than what follows from the above.
Results may differ from a plain program's by a relative error of at most 0.0001.
Values sent between devices are 32-bit elements; how exact they have to be, the bound alone decides.
A program may use at most 128 MiB of HBM per device.

v0:
```python
import jax
import jax.numpy as jnp
from jax import lax
from jax.sharding import PartitionSpec as P

ITERS = 3


epsilon = 1e-06


def in_one(arrays, axis):
    ends = [0]
    for a in arrays:
        ends.append(ends[-1] + a.size)
    so_far = lax.psum(jnp.concatenate([a.ravel() for a in arrays]), axis)
    return tuple((so_far[b:e].reshape(a.shape) for a, b, e in zip(arrays, ends, ends[1:])))


def from_root(block, axis, source):
    block = jnp.where(lax.axis_index(axis) == source, block, jnp.zeros_like(block))
    return lax.psum(block, axis)


def rows_for(lines, peers):
    spare = -len(lines) % peers
    return jnp.pad(lines, [(0, spare)] + [(0, 0)] * (lines.ndim - 1))


def sum_by_parts(array, axis):
    lines = array.reshape(-1, *array.shape[1:][-1:])
    own = lax.psum_scatter(
        rows_for(lines, lax.axis_size(axis)), axis, scatter_dimension=0, tiled=True
    )
    whole = lax.all_gather(own, axis).reshape(-1, *lines.shape[1:])
    return lax.slice_in_dim(whole, 0, len(lines)).reshape(array.shape)


def column_sums(first, second):
    return jnp.sum(first * second, axis=0)


def both_sums(residual, applied):
    return in_one((column_sums(residual, residual), column_sums(residual, applied)), "row")


def on_device(hessian, right_side, mask, damping):
    mask_float = mask.astype(jnp.float32)
    damping_value = damping[0]
    blocks_ratio = lax.axis_size("col") // lax.axis_size("row")
    block_width = hessian.shape[1]
    col_position = lax.axis_index("col")

    def masked_apply(vector):
        own_slice = lax.dynamic_slice_in_dim(
            vector, col_position % blocks_ratio * block_width, block_width, 0
        )
        column_block = from_root(own_slice, "row", col_position // blocks_ratio)
        partial_value = jnp.dot(
            hessian,
            column_block,
            precision=lax.Precision.HIGHEST,
            preferred_element_type=jnp.float32,
        )
        summed = sum_by_parts(partial_value, "col")
        return mask_float * (summed + damping_value * vector)

    residual = mask_float * right_side
    direction = residual
    solution = jnp.zeros_like(right_side)
    applied = masked_apply(residual)
    norm_now, inner = both_sums(residual, applied)
    step_size = norm_now / (inner + epsilon)
    along = applied
    for iteration in range(ITERS):
        solution = solution + step_size * direction
        residual = residual - step_size * along
        if iteration + 1 < ITERS:
            applied = masked_apply(residual)
            norm_next, inner = both_sums(residual, applied)
            factor = norm_next / (norm_now + epsilon)
            curvature = inner - factor * norm_next / step_size
            step_size = norm_next / (curvature + epsilon)
            direction = residual + factor * direction
            along = applied + factor * along
            norm_now = norm_next
    return solution


def solution(mesh):
    in_specs = (P("row", "col"), P("row", None), P("row", None), P())
    out_specs = P("row", None)
    return jax.shard_map(
        on_device, mesh=mesh, in_specs=in_specs, out_specs=out_specs, check_vma=False
    )
```

profile of v0, /device:TPU:1, one launch (start us, length us, event | category | flops | bytes accessed | tf_op | source)
XLA Modules:
  0.0 933.7 jit_solution(12849361006295928117)
XLA Ops:
  15.4 84.3 %all-reduce.4.cloned.1.call-done = f32[1152,512]{1,0:T(8,128)} async-done(((f32[1152,512]{1,0:T(8,128)}), f32[1152,512]{1,0:T(8,128)}) %all-reduce.4.cloned.1.call-update) | async-done | bytes 2359312 | tf_op jit(solution)/shard_map/psum | solution.py:22
  99.7 37.5 %convolution_bitcast_fusion.2 = f32[2304,512]{0,1:T(8,128)} fusion(f32[1152,512]{1,0:T(8,128)} %all-reduce.4.cloned.1.call-done, f32[2304,1152]{1,0:T(8,128)} %param.4), kind=kOutput, calls=%fused_computation.2 | convolution fusion | flops 16307453952 | bytes 17694720 | tf_op jit(solution)/shard_map/dot_general | solution.py:59
  137.2 6.1 copy.11
  143.4 85.0 %reduce-scatter.10.cloned.1.call-done = f32[144,512]{1,0:T(8,128)} async-done(((f32[2304,512]{1,0:T(8,128)}), f32[144,512]{1,0:T(8,128)}) %reduce-scatter.10.cloned.1.call-update) | async-done | bytes 294928 | tf_op jit(solution)/shard_map/reduce_scatter | solution.py:32
  229.4 59.6 %all-gather.7.cloned.1.call-done = f32[2304,512]{1,0:T(8,128)} async-done(((f32[144,512]{1,0:T(8,128)}), f32[2304,512]{1,0:T(8,128)}) %all-gather.7.cloned.1.call-update) | async-done | bytes 4718608 | tf_op jit(solution)/shard_map/all_gather | solution.py:35
  288.9 6.9 multiply_reduce_fusion.5
  295.9 15.1 %psum.43 = f32[1024]{0:T(1024)S(1)} all-reduce(f32[1024]{0:T(1024)S(1)} %pad_maximum_fusion), channel_id=1, replica_groups=mesh['row'=8,'col'=16] {'row'}, use_global_device_ids=true, to_apply=%region_4.5 | all-reduce | flops 1024 | bytes 8192 | tf_op jit(solution)/shard_map/psum | solution.py:16
  311.0 6.9 multiply_subtract_fusion.1
  321.8 80.7 %all-reduce.6.cloned.1.call-done = f32[1152,512]{1,0:T(8,128)} async-done(((f32[1152,512]{1,0:T(8,128)}), f32[1152,512]{1,0:T(8,128)}) %all-reduce.6.cloned.1.call-update) | async-done | bytes 2359312 | tf_op jit(solution)/shard_map/psum | solution.py:22
  402.5 37.5 %convolution_bitcast_fusion.1 = f32[2304,512]{0,1:T(8,128)} fusion(f32[1152,512]{1,0:T(8,128)} %all-reduce.6.cloned.1.call-done, f32[2304,1152]{1,0:T(8,128)} %param.4), kind=kOutput, calls=%fused_computation.1 | convolution fusion | flops 16307453952 | bytes 17694720 | tf_op jit(solution)/shard_map/dot_general | solution.py:59
  446.1 85.0 %reduce-scatter.12.cloned.1.call-done = f32[144,512]{1,0:T(8,128)} async-done(((f32[2304,512]{1,0:T(8,128)}), f32[144,512]{1,0:T(8,128)}) %reduce-scatter.12.cloned.1.call-update) | async-done | bytes 294928 | tf_op jit(solution)/shard_map/reduce_scatter | solution.py:32
  531.1 10.5 %all-reduce.8.cloned.1.call-start = ((), (), s32[]{:S(2)}) async-start(), calls=%async_computation.5 | async-start | bytes 4718592 | tf_op jit(solution)/shard_map/psum | solution.py:22
  541.7 49.5 %all-gather.9.cloned.1.call-done = f32[2304,512]{1,0:T(8,128)} async-done(((f32[144,512]{1,0:T(8,128)}), f32[2304,512]{1,0:T(8,128)}) %all-gather.9.cloned.1.call-update) | async-done | bytes 4718608 | tf_op jit(solution)/shard_map/all_gather | solution.py:35
  591.2 6.9 multiply_reduce_fusion.3
  598.1 15.1 %psum.45 = f32[1024]{0:T(1024)S(1)} all-reduce(f32[1024]{0:T(1024)S(1)} %pad_maximum_fusion.1), channel_id=1, replica_groups=mesh['row'=8,'col'=16] {'row'}, use_global_device_ids=true, to_apply=%region_9.10 | all-reduce | flops 1024 | bytes 8192 | tf_op jit(solution)/shard_map/psum | solution.py:16
  613.3 8.7 multiply_subtract_fusion
  625.9 80.7 %all-reduce.8.cloned.1.call-done = f32[1152,512]{1,0:T(8,128)} async-done(((f32[1152,512]{1,0:T(8,128)}), f32[1152,512]{1,0:T(8,128)}) %all-reduce.8.cloned.1.call-update) | async-done | bytes 2359312 | tf_op jit(solution)/shard_map/psum | solution.py:22
  706.5 37.5 %convolution_bitcast_fusion = f32[2304,512]{0,1:T(8,128)} fusion(f32[1152,512]{1,0:T(8,128)} %all-reduce.8.cloned.1.call-done, f32[2304,1152]{1,0:T(8,128)} %param.4), kind=kOutput, calls=%fused_computation | convolution fusion | flops 16307453952 | bytes 17694720 | tf_op jit(solution)/shard_map/dot_general | solution.py:59
  744.0 6.1 copy.15
  750.4 84.8 %reduce-scatter.14.cloned.1.call-done = f32[144,512]{1,0:T(8,128)} async-done(((f32[2304,512]{1,0:T(8,128)}), f32[144,512]{1,0:T(8,128)}) %reduce-scatter.14.cloned.1.call-update) | async-done | bytes 294928 | tf_op jit(solution)/shard_map/reduce_scatter | solution.py:32
  835.2 60.5 %all-gather.11.cloned.1.call-done = f32[2304,512]{1,0:T(8,128)} async-done(((f32[144,512]{1,0:T(8,128)}), f32[2304,512]{1,0:T(8,128)}) %all-gather.11.cloned.1.call-update) | async-done | bytes 4718608 | tf_op jit(solution)/shard_map/all_gather | solution.py:35
  895.7 6.9 multiply_reduce_fusion.1
  902.6 15.1 %psum.47 = f32[1024]{0:T(1024)S(1)} all-reduce(f32[1024]{0:T(1024)S(1)} %pad_maximum_fusion.2), channel_id=1, replica_groups=mesh['row'=8,'col'=16] {'row'}, use_global_device_ids=true, to_apply=%region_14.15 | all-reduce | flops 1024 | bytes 8192 | tf_op jit(solution)/shard_map/psum | solution.py:16
  917.8 9.2 multiply_add_fusion
  (34 shorter events, 23.5 us)
Async XLA Ops:
  6.5 93.2 %all-reduce.4.cloned.1.call-start = ((), (), s32[]{:S(2)}) async-start(), calls=%async_computation.3 | async-start | bytes 4718592 | tf_op jit(solution)/shard_map/psum | solution.py:22
  11.5 2.2 copy-start
  15.4 213.0 %reduce-scatter.10.cloned.1.call-start = ((), (), s32[]{:S(2)}) async-start(), calls=%async_computation.9 | async-start | bytes 5013504 | tf_op jit(solution)/shard_map/reduce_scatter | solution.py:32
  143.4 145.6 %all-gather.7.cloned.1.call-start = ((), (), s32[]{:S(2)}) async-start(), calls=%async_computation.6 | async-start | bytes 5013504 | tf_op jit(solution)/shard_map/all_gather | solution.py:35
  228.4 174.1 %all-reduce.6.cloned.1.call-start = ((), (), s32[]{:S(2)}) async-start(), calls=%async_computation.4 | async-start | bytes 4718592 | tf_op jit(solution)/shard_map/psum | solution.py:22
  318.0 2.1 copy-start.1
  321.8 209.3 %reduce-scatter.12.cloned.1.call-start = ((), (), s32[]{:S(2)}) async-start(), calls=%async_computation.10 | async-start | bytes 5013504 | tf_op jit(solution)/shard_map/reduce_scatter | solution.py:32
  446.1 145.1 %all-gather.9.cloned.1.call-start = ((), (), s32[]{:S(2)}) async-start(), calls=%async_computation.7 | async-start | bytes 5013504 | tf_op jit(solution)/shard_map/all_gather | solution.py:35
  531.1 175.4 %all-reduce.8.cloned.1.call-start = ((), (), s32[]{:S(2)}) async-start(), calls=%async_computation.5 | async-start | bytes 4718592 | tf_op jit(solution)/shard_map/psum | solution.py:22
  622.0 2.2 copy-start.2
  625.8 209.3 %reduce-scatter.14.cloned.1.call-start = ((), (), s32[]{:S(2)}) async-start(), calls=%async_computation.11 | async-start | bytes 5013504 | tf_op jit(solution)/shard_map/reduce_scatter | solution.py:32
  750.1 145.6 %all-gather.11.cloned.1.call-start = ((), (), s32[]{:S(2)}) async-start(), calls=%async_computation.8 | async-start | bytes 5013504 | tf_op jit(solution)/shard_map/all_gather | solution.py:35
Sparse Core Ops, SparseCore 0:
  15.5 84.1 all-reduce.3
  143.5 84.8 reduce-scatter.9
  231.2 57.7 all-gather.6
  321.9 80.5 all-reduce.5
  446.2 84.8 reduce-scatter.11
  533.4 57.6 all-gather.8
  625.9 80.5 all-reduce.7
  750.2 84.8 reduce-scatter.13
  837.9 57.7 all-gather.10
where the time goes:
time: 946 us; the launch traced here: 934 us
  waiting for transfers between devices  670 us (71%)
  matrix products  112 us (12%)
  other arithmetic  55.5 us (6%)
  blocking collectives  45.4 us (5%)
  local copies, waits for them, and re-layouts  24.8 us (3%)
  between operations  14.1 us (1%)
  starting transfers between devices  11.3 us (1%)
    reduce_scatter x3, waiting for transfers between devices, sum_by_parts(): lax.psum_scatter(rows_for(lines, lax.axis_size(axis)), axis, scatter_dime...  255 us
    psum x3, waiting for transfers between devices, from_root(): return lax.psum(block, axis)  246 us
    all_gather x3, waiting for transfers between devices, sum_by_parts(): whole = lax.all_gather(own, axis).reshape(-1, *lines.shape[1:])  170 us
    dot_general x3, matrix products, masked_apply(): jnp.dot(hessian, column_block, precision=lax.Precision.HIGHEST, preferred...  112 us
    psum x3, blocking collectives, in_one(): so_far = lax.psum(jnp.concatenate([a.ravel() for a in arrays]), axis)  45.4 us
    unnamed x9, local copies, waits for them, and re-layouts  24.8 us
    reduce_sum x3, other arithmetic, column_sums(): return jnp.sum(first * second, axis=0)  20.8 us
  transfers between devices with their start and end apart: 9, of which 9 were waited for; matrix products, arithmetic and copies ran while one was open for 0% of the time, Pallas kernels for 0%

commit v1 on v0

v1 whole, which is shorter than its diff:
```python
import jax
import jax.numpy as jnp
from jax import lax
from jax.experimental import pallas as pl
from jax.experimental.pallas import tpu as pltpu
from jax.sharding import PartitionSpec as P

MESH = pl.DeviceIdType.MESH
F32 = jnp.float32
BF16 = jnp.bfloat16

epsilon = 1e-06

SHARD = 144
QUARTER = 2 * SHARD
WIDTH = 8 * SHARD
ROWS = 16 * SHARD
BLOCK = 4 * SHARD
DEPTH = 256
DEPTHS = ROWS // DEPTH
GROUPS = 2
COPIES = 40
SUMS = 3
PEERS = 10


def halves(value):
    high = value.astype(BF16)
    return high, (value - high.astype(F32)).astype(BF16)


def dot3(a_high, a_low, b_high, b_low, contract):
    dims = ((contract, (0,)), ((), ()))

    def one(a, b):
        return lax.dot_general(a, b, dims, preferred_element_type=F32)

    return one(a_high, b_high) + (one(a_high, b_low) + one(a_low, b_high))


def column_sum(a, b):
    return jnp.sum(a * b, axis=0, keepdims=True)


class Copies:
    def __init__(self, send, receive):
        self.send, self.receive, self.used = send, receive, 0

    def to(self, source, target, device):
        k = self.used
        self.used += 1
        copy = pltpu.make_async_remote_copy(
            src_ref=source,
            dst_ref=target,
            send_sem=self.send.at[k],
            recv_sem=self.receive.at[k],
            device_id=device,
            device_id_type=MESH,
        )
        copy.start()
        return copy


class ToTwin:
    def __init__(self, copies, source, target, place):
        k = copies.used
        copies.used += 1
        self.alone = place["alone"]
        self.remote = pltpu.make_async_remote_copy(
            src_ref=source,
            dst_ref=target,
            send_sem=copies.send.at[k],
            recv_sem=copies.receive.at[k],
            device_id=place["twin"],
            device_id_type=MESH,
        )
        self.local = pltpu.make_async_copy(source, target, copies.receive.at[k])

        @pl.when(self.alone)
        def _():
            self.local.start()

        @pl.when(jnp.logical_not(self.alone))
        def _():
            self.remote.start()

    def wait(self):
        @pl.when(self.alone)
        def _():
            self.local.wait()

        @pl.when(jnp.logical_not(self.alone))
        def _():
            self.remote.wait()


def find_place():
    row, col = lax.axis_index("row"), lax.axis_index("col")
    x_low, z = lax.div(row, 4), lax.rem(row, 4)
    x_high, y, core = lax.div(col, 8), lax.rem(lax.div(col, 2), 4), lax.rem(col, 2)
    row_x, col_x = lax.rem(row + 4, 8), lax.rem(col + 8, 16)
    place = dict(x_low=x_low, z=z, x_high=x_high, y=y, core=core)
    place["z_peers"] = [(x_low * 4 + lax.rem(z + d, 4), col) for d in (1, 2, 3)]
    place["y_peers"] = [(row, x_high * 8 + lax.rem(y + d, 4) * 2 + core) for d in (1, 2, 3)]
    place["x_low_peer"] = (row_x, col)
    place["x_high_peer"] = (row, col_x)
    place["x_peers"] = [(row_x, col), (row, col_x), (row_x, col_x)]
    place["core_peer"] = (row, col + 1 - 2 * core)
    place["twin"] = (x_high * 4 + y, x_low * 8 + z * 2 + core)
    place["alone"] = jnp.logical_and(x_low == x_high, z == y)
    return place


def kernel(
    h_hbm, b_hbm, mask_hbm, damping_ref, out_hbm,
    h_stage, h_high, h_low, mask, r0, r1_rows, r2_rows, cols1, cols2,
    part0, part1, got_z, got_x, got_core, got_y, got_x2, send_x, send_x2,
    r0_own, mask_own, mask_sent, w0_own, w0_rows, w1_rows,
    v_high, v_low, tile_out, tile_in, stage_sem, in_sem, out_sem, send_sem, receive_sem,
):
    groups, _, width = r0.shape
    place = find_place()
    z, y, core, x_low, x_high = (place[k] for k in ("z", "y", "core", "x_low", "x_high"))
    damping = damping_ref[0]

    def load(k, slot):
        return pltpu.make_async_copy(
            h_hbm.at[pl.ds(k * DEPTH, DEPTH), :], h_stage.at[slot], stage_sem.at[slot]
        )

    loads = []
    for g in range(groups):
        columns = pl.ds(g * width, width)
        loads.append(
            (
                pltpu.make_async_copy(b_hbm.at[:, columns], r0.at[g], in_sem.at[2 * g]),
                pltpu.make_async_copy(mask_hbm.at[:, columns], mask.at[g], in_sem.at[2 * g + 1]),
            )
        )
    for pair in loads[:1]:
        for copy in pair:
            copy.start()
    load(0, 0).start()
    load(1, 1).start()
    for pair in loads[1:]:
        for copy in pair:
            copy.start()

    barrier = pltpu.get_barrier_semaphore()
    peers = [*place["z_peers"], *place["y_peers"], *place["x_peers"], place["core_peer"]]
    for peer in peers:
        pl.semaphore_signal(barrier, inc=1, device_id=peer, device_id_type=MESH)

    @pl.when(jnp.logical_not(place["alone"]))
    def _():
        pl.semaphore_signal(barrier, inc=1, device_id=place["twin"], device_id_type=MESH)
        pl.semaphore_wait(barrier, len(peers) + 1)

    @pl.when(place["alone"])
    def _():
        pl.semaphore_wait(barrier, len(peers))

    row_at = pl.multiple_of(core * WIDTH + y * QUARTER + x_high * SHARD, 8)
    col_at = pl.multiple_of(z * QUARTER + x_low * SHARD, 8)
    row_own, col_own = pl.ds(row_at, SHARD), pl.ds(col_at, SHARD)
    twin_own = pl.ds(pl.multiple_of(y * QUARTER + x_high * SHARD, 8), SHARD)
    mine, others = pl.multiple_of(core * WIDTH, 8), pl.multiple_of((1 - core) * WIDTH, 8)

    def first_rows(g):
        @pl.loop(0, 8)
        def _(k):
            at = pl.ds(pl.multiple_of(k * QUARTER, 8), QUARTER)
            r0[g, at, :] = r0[g, at, :] * mask[g, at, :].astype(F32)

    def multiply_first(g, fresh):
        part0[g] = jnp.zeros_like(part0[g])

        @pl.loop(0, DEPTHS)
        def _(k):
            at = pl.ds(pl.multiple_of(k * DEPTH, DEPTH), DEPTH)
            if fresh:
                slot = lax.rem(k, 2)
                load(k, slot).wait()
                high, low = halves(h_stage[slot])
                h_high[at, :] = high
                h_low[at, :] = low

                @pl.when(k < DEPTHS - 2)
                def _():
                    load(k + 2, slot).start()
            b_high, b_low = halves(r0[g, at, :])
            part0[g] += dot3(h_high[at, :], h_low[at, :], b_high, b_low, (0,))

    def split_columns(source, g):
        @pl.loop(0, 4)
        def _(k):
            at = pl.ds(pl.multiple_of(k * QUARTER, 16), QUARTER)
            high, low = halves(source[g, at, :])
            v_high[g, at, :] = high
            v_low[g, at, :] = low

    def multiply_rows(at, g):
        return dot3(h_high[at, :], h_low[at, :], v_high[g], v_low[g], (1,))

    def all_sums(copies, g, s, values):
        lines = width // 128
        steps = ([place["core_peer"]], place["z_peers"], place["y_peers"], place["x_peers"])
        tile_out[g, s, 0] = jnp.zeros((8, 128), F32)
        for v, value in enumerate(values):
            for l in range(lines):
                tile_out[g, s, 0, pl.ds(v * lines + l, 1), :] = value[:, l * 128:(l + 1) * 128]
        slot = 0
        for step, group in enumerate(steps):
            sent = []
            for peer in group:
                sent.append(copies.to(tile_out.at[g, s, step], tile_in.at[g, s, slot], peer))
                slot += 1
            yield
            for copy in sent:
                copy.wait()
            total = tile_out[g, s, step]
            for k in range(slot - len(sent), slot):
                total = total + tile_in[g, s, k]
            if step + 1 < len(steps):
                tile_out[g, s, step + 1] = total
        result = []
        for v in range(len(values)):
            result.append(
                jnp.concatenate([total[v * lines + l:v * lines + l + 1, :] for l in range(lines)], axis=1)
            )
        return result

    def reduce_by(copies, g, source, start, got, quarter, peers_, sent_x, got_last, half, x_peer):
        sent = []
        for d in range(3):
            at = pl.multiple_of(start + lax.rem(quarter + d + 1, 4) * QUARTER, 8)
            sent.append(copies.to(source.at[g, pl.ds(at, QUARTER), :], got.at[g, d], peers_[d]))
        yield
        for copy in sent:
            copy.wait()

        def added(which):
            inner = pl.ds(pl.multiple_of(which * SHARD, 8), SHARD)
            at = pl.ds(pl.multiple_of(start + quarter * QUARTER + which * SHARD, 8), SHARD)
            return (source[g, at, :] + got[g, 0, inner, :]) + (got[g, 1, inner, :] + got[g, 2, inner, :])

        sent_x[g] = added(1 - half)
        last = copies.to(sent_x.at[g], got_last.at[g], x_peer)
        own = added(half)
        yield
        last.wait()
        return own + got_last[g]

    def gather_by(copies, g, whole, own, start, x_peer, peers_):
        first = copies.to(whole.at[g, own, :], whole.at[g, own, :], x_peer)
        yield
        first.wait()
        at = pl.ds(start, QUARTER)
        sent = [copies.to(whole.at[g, at, :], whole.at[g, at, :], peer) for peer in peers_]
        yield
        for copy in sent:
            copy.wait()

    def gather_rows(copies, g, whole):
        start = pl.multiple_of(core * WIDTH + y * QUARTER, 8)
        yield from gather_by(copies, g, whole, row_own, start, place["x_high_peer"], place["y_peers"])
        at = pl.ds(mine, WIDTH)
        last = copies.to(whole.at[g, at, :], whole.at[g, at, :], place["core_peer"])
        yield
        last.wait()

    def gather_columns(copies, g, whole):
        start = pl.multiple_of(z * QUARTER, 8)
        yield from gather_by(copies, g, whole, col_own, start, place["x_low_peer"], place["z_peers"])

    def both(first, second):
        going = [first, second]
        while going:
            for one in list(going):
                try:
                    next(one)
                except StopIteration:
                    going.remove(one)
            if going:
                yield

    def group(g):
        copies = Copies(send_sem.at[g], receive_sem.at[g])
        for copy in loads[g]:
            copy.wait()
        first_rows(g)
        mask_sent[g] = mask[g, row_own, :].astype(F32)
        r0_moved = ToTwin(copies, r0.at[g, row_own, :], r0_own.at[g], place)
        mask_moved = ToTwin(copies, mask_sent.at[g], mask_own.at[g], place)
        multiply_first(g, g == 0)

        summed = yield from reduce_by(
            copies, g, part0, 0, got_z, z, place["z_peers"], send_x, got_x, x_low, place["x_low_peer"]
        )
        r0_moved.wait()
        mask_moved.wait()
        w0_own[g] = mask_own[g] * (summed + damping * r0_own[g])
        w0_moved = ToTwin(copies, w0_own.at[g], w0_rows.at[g], place)
        norm0, curve0 = yield from all_sums(
            copies, g, 0, [column_sum(r0_own[g], r0_own[g]), column_sum(r0_own[g], w0_own[g])]
        )
        step0 = norm0 / (curve0 + epsilon)
        cols1[g, col_own, :] = r0_own[g] - step0 * w0_own[g]
        w0_moved.wait()
        r1 = r0[g, row_own, :] - step0 * w0_rows[g]
        r1_rows[g, row_own, :] = r1

        rest = gather_rows(copies, g, r1_rows)
        column_side = gather_columns(copies, g, cols1)
        for _ in column_side:
            next(rest, None)
            yield
        split_columns(cols1, g)

        for half in (others, mine):
            @pl.loop(0, 2)
            def _(k):
                at = pl.ds(pl.multiple_of(half + k * BLOCK, 16), BLOCK)
                part1[g, at, :] = multiply_rows(at, g)
            if half is others:
                at = pl.ds(others, WIDTH)
                swapped = copies.to(part1.at[g, at, :], got_core.at[g], place["core_peer"])
        yield
        swapped.wait()

        @pl.loop(0, 4)
        def _(k):
            at = pl.ds(pl.multiple_of(mine + k * QUARTER, 8), QUARTER)
            inner = pl.ds(pl.multiple_of(k * QUARTER, 8), QUARTER)
            part1[g, at, :] = part1[g, at, :] + got_core[g, inner, :]

        summed = yield from reduce_by(
            copies, g, part1, mine, got_y, y, place["y_peers"], send_x2, got_x2, x_high, place["x_high_peer"]
        )
        for _ in rest:
            yield
        r1, w0 = r1_rows[g, row_own, :], w0_rows[g]
        w1_rows[g] = mask[g, row_own, :].astype(F32) * (summed + damping * r1)
        norm1, inner1, cross1 = yield from all_sums(
            copies, g, 1, [column_sum(r1, r1), column_sum(r1, w1_rows[g]), column_sum(r1, w0)]
        )
        ratio0 = norm1 / (norm0 + epsilon)
        curve1 = inner1 + ratio0 * (2.0 * cross1 + ratio0 * curve0)
        step1 = norm1 / (curve1 + epsilon)
        along = w1_rows[g] + ratio0 * w0_rows[g]
        r2 = r1_rows[g, row_own, :] - step1 * along
        r2_rows[g, row_own, :] = r2
        norm2, cross2 = column_sum(r2, r2), column_sum(r2, along)
        moved = ToTwin(copies, r2_rows.at[g, row_own, :], cols2.at[g, twin_own, :], place)
        rest = gather_rows(copies, g, r2_rows)
        next(rest, None)
        yield
        moved.wait()
        column_side = gather_columns(copies, g, cols2)
        for _ in column_side:
            next(rest, None)
            yield
        split_columns(cols2, g)

        def dotted(k, total, start):
            at = pl.ds(pl.multiple_of(start + k * BLOCK, 16), BLOCK)
            return total + column_sum(r2_rows[g, at, :], multiply_rows(at, g))

        for _ in rest:
            yield
        inner2 = lax.fori_loop(0, 4, lambda k, total: dotted(k, total, 0), jnp.zeros((1, width), F32))
        norm2, cross2, inner2 = yield from all_sums(copies, g, 2, [norm2, cross2, inner2])
        ratio1 = norm2 / (norm1 + epsilon)
        curve2 = (inner2 + damping * norm2) + ratio1 * (2.0 * cross2 + ratio1 * curve1)
        step2 = norm2 / (curve2 + epsilon)
        on_d1 = step1 + step2 * ratio1

        @pl.loop(0, 8)
        def _(k):
            at = pl.ds(pl.multiple_of(k * QUARTER, 8), QUARTER)
            first = r0[g, at, :]
            d1 = r1_rows[g, at, :] + ratio0 * first
            r0[g, at, :] = step0 * first + on_d1 * d1 + step2 * r2_rows[g, at, :]

        done = pltpu.make_async_copy(r0.at[g], out_hbm.at[:, pl.ds(g * width, width)], out_sem.at[g])
        done.start()
        yield
        done.wait()
        assert copies.used <= COPIES + SUMS * PEERS

    going = [group(g) for g in range(groups)]
    while going:
        for one in list(going):
            try:
                next(one)
            except StopIteration:
                going.remove(one)


def on_device(hessian, right_side, mask, damping):
    rows, columns = right_side.shape
    n, width = GROUPS, columns // GROUPS
    copies = COPIES + SUMS * PEERS

    def many(*shape, dtype=F32):
        return pltpu.VMEM((n, *shape, width), dtype)

    anywhere = pl.BlockSpec(memory_space=pl.ANY)
    return pl.pallas_call(
        kernel,
        out_shape=jax.ShapeDtypeStruct((rows, columns), F32),
        in_specs=[anywhere] * 3 + [pl.BlockSpec(memory_space=pltpu.SMEM)],
        out_specs=anywhere,
        scratch_shapes=[
            pltpu.VMEM((2, DEPTH, WIDTH), F32),
            pltpu.VMEM((ROWS, WIDTH), BF16),
            pltpu.VMEM((ROWS, WIDTH), BF16),
            many(ROWS, dtype=jnp.int32),
            many(ROWS), many(ROWS), many(ROWS), many(WIDTH), many(WIDTH),
            many(WIDTH), many(ROWS), many(3, QUARTER), many(SHARD), many(WIDTH), many(3, QUARTER), many(SHARD),
            many(SHARD), many(SHARD),
            many(SHARD), many(SHARD), many(SHARD), many(SHARD), many(SHARD), many(SHARD),
            many(WIDTH, dtype=BF16), many(WIDTH, dtype=BF16),
            pltpu.VMEM((n, SUMS, 4, 8, 128), F32),
            pltpu.VMEM((n, SUMS, PEERS, 8, 128), F32),
            pltpu.SemaphoreType.DMA((2,)),
            pltpu.SemaphoreType.DMA((2 * n,)),
            pltpu.SemaphoreType.DMA((n,)),
            pltpu.SemaphoreType.DMA((n, copies)),
            pltpu.SemaphoreType.DMA((n, copies)),
        ],
        compiler_params=pltpu.CompilerParams(
            collective_id=0, has_side_effects=True, vmem_limit_bytes=63 << 20
        ),
    )(hessian, right_side, mask, damping)


def solution(mesh):
    in_specs = (P("row", "col"), P("row", None), P("row", None), P())
    return jax.shard_map(
        on_device, mesh=mesh, in_specs=in_specs, out_specs=P("row", None), check_vma=False
    )
```

time: 946 us -> 241 us (0.25); the launches traced: 934 us -> 240 us
  waiting for transfers between devices: 670 us -> 0 us
  Pallas kernels: 0 us -> 234 us
  matrix products: 112 us -> 0 us
  other arithmetic: 55.5 us -> 0 us
  blocking collectives: 45.4 us -> 0 us
  local copies, waits for them, and re-layouts: 24.8 us -> 5.03 us
  between operations: 14.1 us -> 0.66 us
  starting transfers between devices: 11.3 us -> 0 us
    reduce_scatter x3 -> x0, waiting for transfers between devices: 255 us -> none  [sum_by_parts(): lax.psum_scatter(rows_for(lines, lax.axis_size(axis)), axis, scatter_dime...]
    psum x3 -> x0, waiting for transfers between devices: 246 us -> none  [from_root(): return lax.psum(block, axis)]
    pallas_call x0 -> x1, Pallas kernels: none -> 234 us  [on_device(): pl.pallas_call(kernel, out_shape=jax.ShapeDtypeStruct((rows, columns), F3...]
    all_gather x3 -> x0, waiting for transfers between devices: 170 us -> none  [sum_by_parts(): whole = lax.all_gather(own, axis).reshape(-1, *lines.shape[1:])]
    dot_general x3 -> x0, matrix products: 112 us -> none  [masked_apply(): jnp.dot(hessian, column_block, precision=lax.Precision.HIGHEST, preferred...]
    psum x3 -> x0, blocking collectives: 45.4 us -> none  [in_one(): so_far = lax.psum(jnp.concatenate([a.ravel() for a in arrays]), axis)]
    reduce_sum x3 -> x0, other arithmetic: 20.8 us -> none  [column_sums(): return jnp.sum(first * second, axis=0)]
    unnamed x9 -> x1, local copies, waits for them, and re-layouts: 24.8 us -> 5.03 us
  transfers between devices with their start and end apart: 9 -> 0, of which waited for: 9 -> 0; matrix products, arithmetic and copies ran while one was open for 0% -> 0% of each run, Pallas kernels for 0% -> 0%
where the time goes in v1:
time: 241 us; the launch traced here: 240 us
  Pallas kernels  234 us (97%)
  local copies, waits for them, and re-layouts  5.03 us (2%)
    pallas_call x1, Pallas kernels, on_device(): pl.pallas_call(kernel, out_shape=jax.ShapeDtypeStruct((rows, columns), F3...  234 us
    unnamed x1, local copies, waits for them, and re-layouts  5.03 us

profile of v1, /device:TPU:1, one launch (start us, length us, event | category | flops | bytes accessed | tf_op | source)
XLA Modules:
  0.0 239.8 jit_solution(14706929850477262547)
XLA Ops:
  0.7 234.2 %shard_map.46 = f32[2304,512]{1,0:T(8,128)} custom-call(f32[2304,1152]{1,0:T(8,128)} %h_hbm.1, f32[2304,512]{1,0:T(8,128)} %b_hbm.1, s32[2304,512]{1,0:T(8,128)} %mask_hbm.1, f32[1]{0:T(128)S(6)} %copy.6.damping_ref), custom_call_target="tpu_custom_call" | custom-call | tf_op jit(solution)/shard_map/pallas_call | solution.py:409
  234.8 5.0 %copy.7 = f32[2304,512]{1,0:T(8,128)} copy(f32[2304,512]{1,0:T(8,128)} %shard_map.46) | data formatting | bytes 9437184

commit v2 on v1

v2 whole, which is shorter than its diff:
```python
import jax
import jax.numpy as jnp
from jax import lax
from jax.experimental import pallas as pl
from jax.experimental.pallas import tpu as pltpu
from jax.sharding import PartitionSpec as P

MESH = pl.DeviceIdType.MESH
F32 = jnp.float32
BF16 = jnp.bfloat16

epsilon = 1e-06

SHARD = 144
QUARTER = 2 * SHARD
WIDTH = 8 * SHARD
ROWS = 16 * SHARD
BLOCK = 4 * SHARD
DEPTH = 256
DEPTHS = ROWS // DEPTH
GROUPS = 2
COPIES = 48
SUMS = 5
NEAR = 7
FAR = 15


def halves(value):
    high = value.astype(BF16)
    return high, (value - high.astype(F32)).astype(BF16)


def dot3(a_high, a_low, b_high, b_low, contract):
    dims = ((contract, (0,)), ((), ()))

    def one(a, b):
        return lax.dot_general(a, b, dims, preferred_element_type=F32)

    return one(a_high, b_high) + (one(a_high, b_low) + one(a_low, b_high))


def column_sum(a, b):
    return jnp.sum(a * b, axis=0, keepdims=True)


class Copies:
    def __init__(self, send, receive):
        self.send, self.receive, self.used = send, receive, 0

    def to(self, source, target, device):
        k = self.used
        self.used += 1
        copy = pltpu.make_async_remote_copy(
            src_ref=source,
            dst_ref=target,
            send_sem=self.send.at[k],
            recv_sem=self.receive.at[k],
            device_id=device,
            device_id_type=MESH,
        )
        copy.start()
        return copy


class ToTwin:
    def __init__(self, copies, source, target, place):
        k = copies.used
        copies.used += 1
        self.alone = place["alone"]
        self.remote = pltpu.make_async_remote_copy(
            src_ref=source,
            dst_ref=target,
            send_sem=copies.send.at[k],
            recv_sem=copies.receive.at[k],
            device_id=place["twin"],
            device_id_type=MESH,
        )
        self.local = pltpu.make_async_copy(source, target, copies.receive.at[k])

        @pl.when(self.alone)
        def _():
            self.local.start()

        @pl.when(jnp.logical_not(self.alone))
        def _():
            self.remote.start()

    def wait(self):
        @pl.when(self.alone)
        def _():
            self.local.wait()

        @pl.when(jnp.logical_not(self.alone))
        def _():
            self.remote.wait()


def shard_at(start, ring, half):
    return pl.ds(pl.multiple_of(start + ring * QUARTER + half * SHARD, 8), SHARD)


class Reduce:
    def __init__(self, copies, part, relay, got, start, ring, half, device):
        self.copies, self.part, self.relay, self.got = copies, part, relay, got
        self.start, self.ring, self.half, self.device = start, ring, half, device

    def shard(self, step, flip):
        half = 1 - self.half if flip else self.half
        return shard_at(self.start, lax.rem(self.ring + step, 4), half)

    def send(self, step, flip, slot):
        at = self.shard(step, flip)
        return self.copies.to(self.part.at[at, :], self.got.at[slot], self.device(step, flip))

    def first(self):
        up = self.copies.to(self.part.at[self.shard(2, False), :], self.relay.at[0], self.device(1, False))
        down = self.copies.to(self.part.at[self.shard(2, True), :], self.relay.at[1], self.device(3, False))
        self.relays = [up, down]
        self.sent = [self.send(1, True, 1), self.send(3, False, 2), self.send(0, True, 4)]

    def second(self):
        for k, (step, flip) in enumerate(((1, False), (3, True))):
            self.relays[k].wait()
            at = self.shard(step, flip)
            self.part[at, :] = self.part[at, :] + self.relay[k]
            self.sent.append(self.send(step, flip, 3 * k))

    def total(self):
        for copy in self.sent:
            copy.wait()
        got = self.got
        own = self.part[self.shard(0, False), :]
        return ((own + got[0]) + (got[1] + got[2])) + (got[3] + got[4])


class Gather:
    def __init__(self, copies, whole, start, ring, half, device):
        self.copies, self.whole, self.start = copies, whole, start
        self.ring, self.half, self.device = ring, half, device

    def send(self, at, step, flip):
        return self.copies.to(self.whole.at[at, :], self.whole.at[at, :], self.device(step, flip))

    def own(self):
        return shard_at(self.start, self.ring, self.half)

    def forward(self, below, above):
        at = shard_at(self.start, lax.rem(self.ring + 3, 4), self.half)
        below.wait_recv()
        up = self.send(at, 1, False)
        at = shard_at(self.start, lax.rem(self.ring + 1, 4), 1 - self.half)
        above.wait_recv()
        self.last = [up, self.send(at, 3, False)]

    def first(self):
        ways = ((1, False), (3, True), (1, True), (3, False), (0, True))
        self.sent = [self.send(self.own(), *way) for way in ways]

    def second(self):
        self.forward(self.sent[0], self.sent[1])

    def finish(self):
        for copy in self.last:
            copy.wait()
        for k, copy in enumerate(self.sent):
            if k < 2:
                copy.wait_send()
            else:
                copy.wait()


class GatherByAxis(Gather):
    def pair(self):
        self.across = self.send(self.own(), 0, True)

    def first(self):
        self.across.wait()
        at = pl.ds(pl.multiple_of(self.start + self.ring * QUARTER, 8), QUARTER)
        self.sent = [self.send(at, 1, False), self.send(at, 3, False)]

    def swap(self, core_peer):
        for copy in self.last:
            copy.wait()
        for copy in self.sent:
            copy.wait_send()
        at = pl.ds(self.start, WIDTH)
        self.half_sent = self.copies.to(self.whole.at[at, :], self.whole.at[at, :], core_peer)

    def finish(self):
        self.half_sent.wait()


class AllSums:
    def __init__(self, tile_out, tile_in, send, receive, place):
        self.tile_out, self.tile_in, self.copies = tile_out, tile_in, Copies(send, receive)
        self.near, self.far = place["near"], place["far"]

    def first(self, lines):
        self.tile_out[0] = jnp.zeros((8, 128), F32)
        for k, line in enumerate(lines):
            self.tile_out[0, pl.ds(k, 1), :] = line
        self.send(0, self.near)

    def send(self, step, peers):
        self.sent = []
        for peer in peers:
            k = self.copies.used
            self.sent.append(self.copies.to(self.tile_out.at[step], self.tile_in.at[k], peer))

    def added(self, step):
        for copy in self.sent:
            copy.wait()
        total = self.tile_out[step]
        for k in range(self.copies.used - len(self.sent), self.copies.used):
            total = total + self.tile_in[k]
        return total

    def second(self):
        self.tile_out[1] = self.added(0)
        self.send(1, self.far)

    def total(self):
        return self.added(1)


def lines_of(value):
    return [value[:, k * 128:(k + 1) * 128] for k in range(value.shape[1] // 128)]


def value_of(tile, first, count):
    return jnp.concatenate([tile[k:k + 1, :] for k in range(first, first + count)], axis=1)


def find_place():
    row, col = lax.axis_index("row"), lax.axis_index("col")
    x_low, z = lax.div(row, 4), lax.rem(row, 4)
    x_high, y, core = lax.div(col, 8), lax.rem(lax.div(col, 2), 4), lax.rem(col, 2)
    place = dict(x_low=x_low, z=z, x_high=x_high, y=y, core=core)

    def device(dz=0, dy=0, low=0, high=0, dcore=0):
        at_z, at_y = lax.rem(z + dz, 4), lax.rem(y + dy, 4)
        at_low = 1 - x_low if low else x_low
        at_high = 1 - x_high if high else x_high
        at_core = 1 - core if dcore else core
        return (at_low * 4 + at_z, at_high * 8 + at_y * 2 + at_core)

    place["on_row"] = lambda step, flip: device(dz=step, low=flip)
    place["on_col"] = lambda step, flip: device(dy=step, high=flip)
    place["core_peer"] = device(dcore=1)
    place["near"] = [
        device(low=a, high=b, dcore=c) for a in (0, 1) for b in (0, 1) for c in (0, 1) if a + b + c
    ]
    place["far"] = [device(dz=a, dy=b) for a in range(4) for b in range(4) if a + b]
    place["other"] = [device(dz=d, low=1) for d in (1, 3)] + [device(dy=d, high=1) for d in (1, 3)]
    place["twin"] = (x_high * 4 + y, x_low * 8 + z * 2 + core)
    place["alone"] = jnp.logical_and(x_low == x_high, z == y)
    return place


def kernel(
    h_hbm, b_hbm, mask_hbm, damping_ref, out_hbm,
    h_stage, h_high, h_low, mask, r0, w0_rows, r2_rows, cols1, cols2,
    part0, part1, relay0, got0, relay1, got1, got_core,
    r0_own, mask_own, mask_sent,
    v_high, v_low, tile_out, tile_in, stage_sem, in_sem, out_sem, send_sem, receive_sem,
    sums_send, sums_receive,
):
    groups, _, width = r0.shape
    place = find_place()
    z, y, core, x_low, x_high = (place[k] for k in ("z", "y", "core", "x_low", "x_high"))
    core_peer = place["core_peer"]
    damping = damping_ref[0]

    def load(k, slot):
        return pltpu.make_async_copy(
            h_hbm.at[pl.ds(k * DEPTH, DEPTH), :], h_stage.at[slot], stage_sem.at[slot]
        )

    loads = []
    for g in range(groups):
        columns = pl.ds(g * width, width)
        loads.append(
            (
                pltpu.make_async_copy(b_hbm.at[:, columns], r0.at[g], in_sem.at[2 * g]),
                pltpu.make_async_copy(mask_hbm.at[:, columns], mask.at[g], in_sem.at[2 * g + 1]),
            )
        )
    for copy in loads[0]:
        copy.start()
    load(0, 0).start()
    load(1, 1).start()
    for copy in loads[1]:
        copy.start()

    barrier = pltpu.get_barrier_semaphore()
    peers = [*place["near"], *place["far"], *place["other"]]
    for peer in peers:
        pl.semaphore_signal(barrier, inc=1, device_id=peer, device_id_type=MESH)

    @pl.when(jnp.logical_not(place["alone"]))
    def _():
        pl.semaphore_signal(barrier, inc=1, device_id=place["twin"], device_id_type=MESH)

    mine, others = pl.multiple_of(core * WIDTH, 8), pl.multiple_of((1 - core) * WIDTH, 8)
    row_own, col_own = shard_at(mine, y, x_high), shard_at(0, z, x_low)
    twin_row, twin_col = shard_at(mine, z, x_low), shard_at(0, y, x_high)

    def first_rows(g):
        for copy in loads[g]:
            copy.wait()

        @pl.loop(0, 8)
        def _(k):
            at = pl.ds(pl.multiple_of(k * QUARTER, 8), QUARTER)
            r0[g, at, :] = r0[g, at, :] * mask[g, at, :].astype(F32)

        mask_sent[g] = mask[g, row_own, :].astype(F32)

    def multiply_first(g, fresh):
        part0[g] = jnp.zeros_like(part0[g])

        @pl.loop(0, DEPTHS)
        def _(k):
            at = pl.ds(pl.multiple_of(k * DEPTH, DEPTH), DEPTH)
            if fresh:
                slot = lax.rem(k, 2)
                load(k, slot).wait()
                high, low = halves(h_stage[slot])
                h_high[at, :] = high
                h_low[at, :] = low

                @pl.when(k < DEPTHS - 2)
                def _():
                    load(k + 2, slot).start()
            b_high, b_low = halves(r0[g, at, :])
            part0[g] += dot3(h_high[at, :], h_low[at, :], b_high, b_low, (0,))

    def split_columns(source, g):
        @pl.loop(0, 4)
        def _(k):
            at = pl.ds(pl.multiple_of(k * QUARTER, 16), QUARTER)
            high, low = halves(source[g, at, :])
            v_high[g, at, :] = high
            v_low[g, at, :] = low

    def multiply_rows(at, g):
        return dot3(h_high[at, :], h_low[at, :], v_high[g], v_low[g], (1,))

    def multiply_block(g, half, k):
        at = pl.ds(pl.multiple_of(half + k * BLOCK, 16), BLOCK)
        part1[g, at, :] = multiply_rows(at, g)

    both = range(groups)
    copies = [Copies(send_sem.at[g], receive_sem.at[g]) for g in both]
    reduce_row = [
        Reduce(copies[g], part0.at[g], relay0.at[g], got0.at[g], 0, z, x_low, place["on_row"]) for g in both
    ]
    reduce_col = [
        Reduce(copies[g], part1.at[g], relay1.at[g], got1.at[g], mine, y, x_high, place["on_col"]) for g in both
    ]
    gather_w0 = [Gather(copies[g], cols1.at[g], 0, z, x_low, place["on_row"]) for g in both]
    gather_r2 = [Gather(copies[g], cols2.at[g], 0, z, x_low, place["on_row"]) for g in both]
    rows_w0 = [GatherByAxis(copies[g], w0_rows.at[g], mine, y, x_high, place["on_col"]) for g in both]
    rows_r2 = [GatherByAxis(copies[g], r2_rows.at[g], mine, y, x_high, place["on_col"]) for g in both]
    sums = [
        AllSums(tile_out.at[s], tile_in.at[s], sums_send.at[s], sums_receive.at[s], place) for s in range(SUMS)
    ]
    lines = width // 128
    moved, w0_moved, r2_moved, swaps, dots0 = {}, {}, {}, {}, {}

    def send_to_twin(g):
        moved[g] = [
            ToTwin(copies[g], r0.at[g, row_own, :], r0_own.at[g], place),
            ToTwin(copies[g], mask_sent.at[g], mask_own.at[g], place),
        ]

    def end_first(g):
        summed = reduce_row[g].total()
        for copy in moved[g]:
            copy.wait()
        r0_here = r0_own[g]
        w0 = mask_own[g] * (summed + damping * r0_here)
        cols1[g, col_own, :] = w0
        gather_w0[g].first()
        w0_moved[g] = ToTwin(copies[g], cols1.at[g, col_own, :], w0_rows.at[g, twin_row, :], place)
        dots0[g] = (column_sum(r0_here, r0_here), column_sum(r0_here, w0))

    def send_other_half(g):
        swaps[g] = []
        pl.loop(0, 2)(lambda k: multiply_block(g, others, k))
        for k in range(2):
            at = pl.ds(pl.multiple_of(others + k * BLOCK, 16), BLOCK)
            inner = pl.ds(k * BLOCK, BLOCK)
            swaps[g].append(copies[g].to(part1.at[g, at, :], got_core.at[g, inner, :], core_peer))

    def add_other_core(g):
        for copy in swaps[g]:
            copy.wait()

        @pl.loop(0, 4)
        def _(k):
            at = pl.ds(pl.multiple_of(mine + k * QUARTER, 8), QUARTER)
            inner = pl.ds(pl.multiple_of(k * QUARTER, 8), QUARTER)
            part1[g, at, :] = part1[g, at, :] + got_core[g, inner, :]

        reduce_col[g].first()

    def sums_of(s, values):
        sums[s].first([line for value in values for line in lines_of(value)])

    shards = {}

    def end_second(g):
        summed = reduce_col[g].total()
        r0_here, w0 = r0[g, row_own, :], w0_rows[g, row_own, :]
        r1 = r0_here - step0[g] * w0
        w1 = w0 - step0[g] * (mask_sent[g] * (summed + damping * w0))
        r2_rows[g, row_own, :] = w1
        sums_of(1 + g, [column_sum(r1, r1), column_sum(r1, w1), column_sum(r1, w0)])

    def make_r2(g):
        tile = sums[1 + g].total()
        norm1, inner1, cross1 = (value_of(tile, k * lines, lines) for k in range(3))
        ratio0 = norm1 / (norm0[g] + epsilon)
        curve1 = inner1 + ratio0 * (2.0 * cross1 + ratio0 * curve0[g])
        step1 = norm1 / (curve1 + epsilon)
        w0 = w0_rows[g, row_own, :]
        along = r2_rows[g, row_own, :] + ratio0 * w0
        r2 = (r0[g, row_own, :] - step0[g] * w0) - step1 * along
        r2_rows[g, row_own, :] = r2
        r2_moved[g] = ToTwin(copies[g], r2_rows.at[g, row_own, :], cols2.at[g, twin_col, :], place)
        rows_r2[g].pair()
        shards[g] = (norm1, ratio0, curve1, step1, column_sum(r2, r2), column_sum(r2, along))

    def dotted(g, half):
        def one(k, total):
            at = pl.ds(pl.multiple_of(half + k * BLOCK, 16), BLOCK)
            return total + column_sum(r2_rows[g, at, :], multiply_rows(at, g))

        return lax.fori_loop(0, 2, one, jnp.zeros((1, width), F32))

    def finish(g):
        tile = sums[3 + g].total()
        norm2, cross2, inner2 = (value_of(tile, k * lines, lines) for k in range(3))
        norm1, ratio0, curve1, step1, _, _ = shards[g]
        ratio1 = norm2 / (norm1 + epsilon)
        curve2 = (inner2 + damping * norm2) + ratio1 * (2.0 * cross2 + ratio1 * curve1)
        step2 = norm2 / (curve2 + epsilon)
        on_d1 = step1 + step2 * ratio1
        on_r0 = step0[g] + on_d1 * (1.0 + ratio0)
        on_w0 = on_d1 * step0[g]

        @pl.loop(0, 8)
        def _(k):
            at = pl.ds(pl.multiple_of(k * QUARTER, 8), QUARTER)
            r0[g, at, :] = (on_r0 * r0[g, at, :] - on_w0 * w0_rows[g, at, :]) + step2 * r2_rows[g, at, :]

        done = pltpu.make_async_copy(r0.at[g], out_hbm.at[:, pl.ds(g * width, width)], out_sem.at[g])
        done.start()
        return done

    first_rows(0)

    @pl.when(jnp.logical_not(place["alone"]))
    def _():
        pl.semaphore_wait(barrier, len(peers) + 1)

    @pl.when(place["alone"])
    def _():
        pl.semaphore_wait(barrier, len(peers))

    send_to_twin(0)
    multiply_first(0, True)
    reduce_row[0].first()
    first_rows(1)
    send_to_twin(1)
    multiply_first(1, False)
    reduce_row[0].second()
    reduce_row[1].first()
    end_first(0)
    reduce_row[1].second()
    gather_w0[0].second()
    w0_moved[0].wait()
    rows_w0[0].pair()
    end_first(1)
    sums_of(0, [dots0[0][0], dots0[1][0], dots0[0][1], dots0[1][1]])
    rows_w0[0].first()
    gather_w0[0].finish()
    split_columns(cols1, 0)
    send_other_half(0)
    gather_w0[1].second()
    sums[0].second()
    rows_w0[0].forward(*rows_w0[0].sent)
    pl.loop(0, 2)(lambda k: multiply_block(0, mine, k))
    add_other_core(0)
    w0_moved[1].wait()
    rows_w0[1].pair()
    gather_w0[1].finish()
    split_columns(cols1, 1)
    reduce_col[0].second()
    rows_w0[1].first()
    send_other_half(1)
    tile = sums[0].total()
    norm0 = [value_of(tile, g * lines, lines) for g in both]
    curve0 = [value_of(tile, (2 + g) * lines, lines) for g in both]
    step0 = [norm0[g] / (curve0[g] + epsilon) for g in both]
    rows_w0[0].swap(core_peer)
    pl.loop(0, 2)(lambda k: multiply_block(1, mine, k))
    add_other_core(1)
    rows_w0[1].forward(*rows_w0[1].sent)
    end_second(0)
    reduce_col[1].second()
    sums[1].second()
    end_second(1)
    make_r2(0)
    sums[2].second()
    r2_moved[0].wait()
    gather_r2[0].first()
    rows_r2[0].first()
    make_r2(1)
    gather_r2[0].second()
    rows_r2[0].forward(*rows_r2[0].sent)
    rows_w0[1].swap(core_peer)
    r2_moved[1].wait()
    gather_r2[1].first()
    rows_r2[1].first()
    gather_r2[0].finish()
    rows_r2[0].swap(core_peer)
    split_columns(cols2, 0)
    inner2 = dotted(0, mine)
    gather_r2[1].second()
    rows_r2[1].forward(*rows_r2[1].sent)
    rows_r2[0].finish()
    sums_of(3, [*shards[0][4:], inner2 + dotted(0, others)])
    gather_r2[1].finish()
    rows_r2[1].swap(core_peer)
    split_columns(cols2, 1)
    sums[3].second()
    inner2 = dotted(1, mine)
    rows_r2[1].finish()
    sums_of(4, [*shards[1][4:], inner2 + dotted(1, others)])
    rows_w0[0].finish()
    rows_w0[1].finish()
    last = [finish(0)]
    sums[4].second()
    last.append(finish(1))
    for copy in last:
        copy.wait()


def on_device(hessian, right_side, mask, damping):
    rows, columns = right_side.shape
    n, width = GROUPS, columns // GROUPS

    def many(*shape, dtype=F32):
        return pltpu.VMEM((n, *shape, width), dtype)

    anywhere = pl.BlockSpec(memory_space=pl.ANY)
    return pl.pallas_call(
        kernel,
        out_shape=jax.ShapeDtypeStruct((rows, columns), F32),
        in_specs=[anywhere] * 3 + [pl.BlockSpec(memory_space=pltpu.SMEM)],
        out_specs=anywhere,
        scratch_shapes=[
            pltpu.VMEM((2, DEPTH, WIDTH), F32),
            pltpu.VMEM((ROWS, WIDTH), BF16),
            pltpu.VMEM((ROWS, WIDTH), BF16),
            many(ROWS, dtype=jnp.int32),
            many(ROWS), many(ROWS), many(ROWS), many(WIDTH), many(WIDTH),
            many(WIDTH), many(ROWS),
            many(2, SHARD), many(5, SHARD), many(2, SHARD), many(5, SHARD), many(WIDTH),
            many(SHARD), many(SHARD), many(SHARD),
            many(WIDTH, dtype=BF16), many(WIDTH, dtype=BF16),
            pltpu.VMEM((SUMS, 2, 8, 128), F32),
            pltpu.VMEM((SUMS, NEAR + FAR, 8, 128), F32),
            pltpu.SemaphoreType.DMA((2,)),
            pltpu.SemaphoreType.DMA((2 * n,)),
            pltpu.SemaphoreType.DMA((n,)),
            pltpu.SemaphoreType.DMA((n, COPIES)),
            pltpu.SemaphoreType.DMA((n, COPIES)),
            pltpu.SemaphoreType.DMA((SUMS, NEAR + FAR)),
            pltpu.SemaphoreType.DMA((SUMS, NEAR + FAR)),
        ],
        compiler_params=pltpu.CompilerParams(
            collective_id=0, has_side_effects=True, vmem_limit_bytes=63 << 20
        ),
    )(hessian, right_side, mask, damping)


def solution(mesh):
    in_specs = (P("row", "col"), P("row", None), P("row", None), P())
    return jax.shard_map(
        on_device, mesh=mesh, in_specs=in_specs, out_specs=P("row", None), check_vma=False
    )
```

time: 241 us -> 191 us (0.79)
  Pallas kernels: 234 us -> 185 us
    pallas_call x1, Pallas kernels: 234 us -> 185 us  [on_device(): pl.pallas_call(kernel, out_shape=jax.ShapeDtypeStruct((rows, columns), F3...]
where the time goes in v2:
time: 191 us
  Pallas kernels  185 us (97%)
  local copies, waits for them, and re-layouts  5.03 us (3%)
    pallas_call x1, Pallas kernels, on_device(): pl.pallas_call(kernel, out_shape=jax.ShapeDtypeStruct((rows, columns), F3...  185 us
    unnamed x1, local copies, waits for them, and re-layouts  5.03 us

profile of v2, /device:TPU:1, one launch (start us, length us, event | category | flops | bytes accessed | tf_op | source)
XLA Modules:
  0.0 190.7 jit_solution(2174734053906095684)
XLA Ops:
  0.7 185.0 %shard_map.46 = f32[2304,512]{1,0:T(8,128)} custom-call(f32[2304,1152]{1,0:T(8,128)} %h_hbm.1, f32[2304,512]{1,0:T(8,128)} %b_hbm.1, s32[2304,512]{1,0:T(8,128)} %mask_hbm.1, f32[1]{0:T(128)S(6)} %copy.6.damping_ref), custom_call_target="tpu_custom_call" | custom-call | tf_op jit(solution)/shard_map/pallas_call | solution.py:559
  185.7 5.0 %copy.7 = f32[2304,512]{1,0:T(8,128)} copy(f32[2304,512]{1,0:T(8,128)} %shard_map.46) | data formatting | bytes 9437184

commit v3 on v2

--- a/solution.py
+++ b/solution.py
@@ -261,7 +261,7 @@
     h_hbm, b_hbm, mask_hbm, damping_ref, out_hbm,
     h_stage, h_high, h_low, mask, r0, w0_rows, r2_rows, cols1, cols2,
     part0, part1, relay0, got0, relay1, got1, got_core,
-    r0_own, mask_own, mask_sent,
+    b_own, mask_own, mask_sent,
     v_high, v_low, tile_out, tile_in, stage_sem, in_sem, out_sem, send_sem, receive_sem,
     sums_send, sums_receive,
 ):
@@ -366,20 +366,17 @@
         AllSums(tile_out.at[s], tile_in.at[s], sums_send.at[s], sums_receive.at[s], place) for s in range(SUMS)
     ]
     lines = width // 128
-    moved, w0_moved, r2_moved, swaps, dots0 = {}, {}, {}, {}, {}
-
-    def send_to_twin(g):
-        moved[g] = [
-            ToTwin(copies[g], r0.at[g, row_own, :], r0_own.at[g], place),
-            ToTwin(copies[g], mask_sent.at[g], mask_own.at[g], place),
-        ]
+    w0_moved, r2_moved, swaps, dots0 = {}, {}, {}, {}
 
     def end_first(g):
         summed = reduce_row[g].total()
-        for copy in moved[g]:
-            copy.wait()
-        r0_here = r0_own[g]
-        w0 = mask_own[g] * (summed + damping * r0_here)
+        if g == 0:
+            for copy in moved:
+                copy.wait()
+        columns = pl.ds(g * width, width)
+        keep = mask_own[:, columns].astype(F32)
+        r0_here = keep * b_own[:, columns]
+        w0 = keep * (summed + damping * r0_here)
         cols1[g, col_own, :] = w0
         gather_w0[g].first()
         w0_moved[g] = ToTwin(copies[g], cols1.at[g, col_own, :], w0_rows.at[g, twin_row, :], place)
@@ -459,8 +456,6 @@
         done.start()
         return done
 
-    first_rows(0)
-
     @pl.when(jnp.logical_not(place["alone"]))
     def _():
         pl.semaphore_wait(barrier, len(peers) + 1)
@@ -469,11 +464,14 @@
     def _():
         pl.semaphore_wait(barrier, len(peers))
 
-    send_to_twin(0)
+    moved = [
+        ToTwin(copies[0], b_hbm.at[row_own, :], b_own, place),
+        ToTwin(copies[0], mask_hbm.at[row_own, :], mask_own, place),
+    ]
+    first_rows(0)
     multiply_first(0, True)
     reduce_row[0].first()
     first_rows(1)
-    send_to_twin(1)
     multiply_first(1, False)
     reduce_row[0].second()
     reduce_row[1].first()
@@ -569,7 +567,7 @@
             many(ROWS), many(ROWS), many(ROWS), many(WIDTH), many(WIDTH),
             many(WIDTH), many(ROWS),
             many(2, SHARD), many(5, SHARD), many(2, SHARD), many(5, SHARD), many(WIDTH),
-            many(SHARD), many(SHARD), many(SHARD),
+            pltpu.VMEM((SHARD, columns), F32), pltpu.VMEM((SHARD, columns), jnp.int32), many(SHARD),
             many(WIDTH, dtype=BF16), many(WIDTH, dtype=BF16),
             pltpu.VMEM((SUMS, 2, 8, 128), F32),
             pltpu.VMEM((SUMS, NEAR + FAR, 8, 128), F32),

time: 191 us -> 191 us (level)
  no operation moved by 1% of the time
where the time goes in v3:
time: 191 us; the launch traced here: 190 us
  Pallas kernels  185 us (97%)
  local copies, waits for them, and re-layouts  5.03 us (3%)
    pallas_call x1, Pallas kernels, on_device(): pl.pallas_call(kernel, out_shape=jax.ShapeDtypeStruct((rows, columns), F3...  185 us
    unnamed x1, local copies, waits for them, and re-layouts  5.03 us

profile of v3, /device:TPU:1, one launch (start us, length us, event | category | flops | bytes accessed | tf_op | source)
XLA Modules:
  0.0 190.2 jit_solution(9091843039399239637)
XLA Ops:
  0.7 184.5 %shard_map.46 = f32[2304,512]{1,0:T(8,128)} custom-call(f32[2304,1152]{1,0:T(8,128)} %h_hbm.1, f32[2304,512]{1,0:T(8,128)} %b_hbm.1, s32[2304,512]{1,0:T(8,128)} %mask_hbm.1, f32[1]{0:T(128)S(6)} %copy.6.damping_ref), custom_call_target="tpu_custom_call" | custom-call | tf_op jit(solution)/shard_map/pallas_call | solution.py:557
  185.2 5.0 %copy.7 = f32[2304,512]{1,0:T(8,128)} copy(f32[2304,512]{1,0:T(8,128)} %shard_map.46) | data formatting | bytes 9437184

commit v4 on v3

--- a/solution.py
+++ b/solution.py
@@ -63,16 +63,16 @@
 
 
 class ToTwin:
-    def __init__(self, copies, source, target, place):
+    def __init__(self, copies, source, target, device, alone):
         k = copies.used
         copies.used += 1
-        self.alone = place["alone"]
+        self.alone = alone
         self.remote = pltpu.make_async_remote_copy(
             src_ref=source,
             dst_ref=target,
             send_sem=copies.send.at[k],
             recv_sem=copies.receive.at[k],
-            device_id=place["twin"],
+            device_id=device,
             device_id_type=MESH,
         )
         self.local = pltpu.make_async_copy(source, target, copies.receive.at[k])
@@ -252,8 +252,21 @@
     ]
     place["far"] = [device(dz=a, dy=b) for a in range(4) for b in range(4) if a + b]
     place["other"] = [device(dz=d, low=1) for d in (1, 3)] + [device(dy=d, high=1) for d in (1, 3)]
-    place["twin"] = (x_high * 4 + y, x_low * 8 + z * 2 + core)
-    place["alone"] = jnp.logical_and(x_low == x_high, z == y)
+    ring, half = lax.rem(z + core, 4), lax.rem(x_low + core, 2)
+    place["ring"], place["half"] = ring, half
+    to_half = lax.rem(x_high + core, 2)
+
+    def to_columns(turn, flip):
+        at_low = 1 - to_half if flip else to_half
+        return (at_low * 4 + lax.rem(y + 8 - core - turn, 4), x_low * 8 + z * 2 + core)
+
+    def to_rows(turn, flip):
+        at_high = 1 - half if flip else half
+        return (x_high * 4 + y, at_high * 8 + lax.rem(ring + turn, 4) * 2 + core)
+
+    place["to_columns"], place["to_rows"] = to_columns(0, False), to_rows(0, False)
+    place["mask_to"], place["mask_from"] = to_columns(2, True), to_rows(2, True)
+    place["alone"] = jnp.logical_and(jnp.logical_and(x_low == x_high, z == y), core == 0)
     return place
 
 
@@ -293,17 +306,21 @@
         copy.start()
 
     barrier = pltpu.get_barrier_semaphore()
-    peers = [*place["near"], *place["far"], *place["other"]]
+    peers = [*place["near"], *place["far"], *place["other"], place["mask_from"]]
     for peer in peers:
         pl.semaphore_signal(barrier, inc=1, device_id=peer, device_id_type=MESH)
 
     @pl.when(jnp.logical_not(place["alone"]))
     def _():
-        pl.semaphore_signal(barrier, inc=1, device_id=place["twin"], device_id_type=MESH)
+        for peer in (place["to_rows"], place["to_columns"]):
+            pl.semaphore_signal(barrier, inc=1, device_id=peer, device_id_type=MESH)
 
     mine, others = pl.multiple_of(core * WIDTH, 8), pl.multiple_of((1 - core) * WIDTH, 8)
-    row_own, col_own = shard_at(mine, y, x_high), shard_at(0, z, x_low)
-    twin_row, twin_col = shard_at(mine, z, x_low), shard_at(0, y, x_high)
+    ring, half = place["ring"], place["half"]
+    row_own, col_own = shard_at(mine, y, x_high), shard_at(0, ring, half)
+    twin_row, twin_col = shard_at(mine, ring, half), shard_at(0, y, x_high)
+    mask_rows = shard_at(mine, lax.rem(y + 2, 4), 1 - x_high)
+    alone = place["alone"]
 
     def first_rows(g):
         for copy in loads[g]:
@@ -353,13 +370,13 @@
     both = range(groups)
     copies = [Copies(send_sem.at[g], receive_sem.at[g]) for g in both]
     reduce_row = [
-        Reduce(copies[g], part0.at[g], relay0.at[g], got0.at[g], 0, z, x_low, place["on_row"]) for g in both
+        Reduce(copies[g], part0.at[g], relay0.at[g], got0.at[g], 0, ring, half, place["on_row"]) for g in both
     ]
     reduce_col = [
         Reduce(copies[g], part1.at[g], relay1.at[g], got1.at[g], mine, y, x_high, place["on_col"]) for g in both
     ]
-    gather_w0 = [Gather(copies[g], cols1.at[g], 0, z, x_low, place["on_row"]) for g in both]
-    gather_r2 = [Gather(copies[g], cols2.at[g], 0, z, x_low, place["on_row"]) for g in both]
+    gather_w0 = [Gather(copies[g], cols1.at[g], 0, ring, half, place["on_row"]) for g in both]
+    gather_r2 = [Gather(copies[g], cols2.at[g], 0, ring, half, place["on_row"]) for g in both]
     rows_w0 = [GatherByAxis(copies[g], w0_rows.at[g], mine, y, x_high, place["on_col"]) for g in both]
     rows_r2 = [GatherByAxis(copies[g], r2_rows.at[g], mine, y, x_high, place["on_col"]) for g in both]
     sums = [
@@ -379,7 +396,8 @@
         w0 = keep * (summed + damping * r0_here)
         cols1[g, col_own, :] = w0
         gather_w0[g].first()
-        w0_moved[g] = ToTwin(copies[g], cols1.at[g, col_own, :], w0_rows.at[g, twin_row, :], place)
+        here, there = cols1.at[g, col_own, :], w0_rows.at[g, twin_row, :]
+        w0_moved[g] = ToTwin(copies[g], here, there, place["to_rows"], alone)
         dots0[g] = (column_sum(r0_here, r0_here), column_sum(r0_here, w0))
 
     def send_other_half(g):
@@ -425,7 +443,8 @@
         along = r2_rows[g, row_own, :] + ratio0 * w0
         r2 = (r0[g, row_own, :] - step0[g] * w0) - step1 * along
         r2_rows[g, row_own, :] = r2
-        r2_moved[g] = ToTwin(copies[g], r2_rows.at[g, row_own, :], cols2.at[g, twin_col, :], place)
+        here, there = r2_rows.at[g, row_own, :], cols2.at[g, twin_col, :]
+        r2_moved[g] = ToTwin(copies[g], here, there, place["to_columns"], alone)
         rows_r2[g].pair()
         shards[g] = (norm1, ratio0, curve1, step1, column_sum(r2, r2), column_sum(r2, along))
 
@@ -458,15 +477,15 @@
 
     @pl.when(jnp.logical_not(place["alone"]))
     def _():
-        pl.semaphore_wait(barrier, len(peers) + 1)
+        pl.semaphore_wait(barrier, len(peers) + 2)
 
     @pl.when(place["alone"])
     def _():
         pl.semaphore_wait(barrier, len(peers))
 
     moved = [
-        ToTwin(copies[0], b_hbm.at[row_own, :], b_own, place),
-        ToTwin(copies[0], mask_hbm.at[row_own, :], mask_own, place),
+        ToTwin(copies[0], b_hbm.at[row_own, :], b_own, place["to_columns"], alone),
+        copies[0].to(mask_hbm.at[mask_rows, :], mask_own, place["mask_to"]),
     ]
     first_rows(0)
     multiply_first(0, True)

time: 191 us -> 191 us (level)
  no operation moved by 1% of the time
where the time goes in v4:
time: 191 us; the launch traced here: 190 us
  Pallas kernels  185 us (97%)
  local copies, waits for them, and re-layouts  5.03 us (3%)
    pallas_call x1, Pallas kernels, on_device(): pl.pallas_call(kernel, out_shape=jax.ShapeDtypeStruct((rows, columns), F3...  185 us
    unnamed x1, local copies, waits for them, and re-layouts  5.03 us

profile of v4, /device:TPU:1, one launch (start us, length us, event | category | flops | bytes accessed | tf_op | source)
XLA Modules:
  0.0 190.4 jit_solution(739138396603793854)
XLA Ops:
  0.7 184.7 %shard_map.46 = f32[2304,512]{1,0:T(8,128)} custom-call(f32[2304,1152]{1,0:T(8,128)} %h_hbm.1, f32[2304,512]{1,0:T(8,128)} %b_hbm.1, s32[2304,512]{1,0:T(8,128)} %mask_hbm.1, f32[1]{0:T(128)S(6)} %copy.6.damping_ref), custom_call_target="tpu_custom_call" | custom-call | tf_op jit(solution)/shard_map/pallas_call | solution.py:576
  185.4 5.0 %copy.7 = f32[2304,512]{1,0:T(8,128)} copy(f32[2304,512]{1,0:T(8,128)} %shard_map.46) | data formatting | bytes 9437184

commit v5 on v4

--- a/solution.py
+++ b/solution.py
@@ -256,16 +256,8 @@
     place["ring"], place["half"] = ring, half
     to_half = lax.rem(x_high + core, 2)
 
-    def to_columns(turn, flip):
-        at_low = 1 - to_half if flip else to_half
-        return (at_low * 4 + lax.rem(y + 8 - core - turn, 4), x_low * 8 + z * 2 + core)
-
-    def to_rows(turn, flip):
-        at_high = 1 - half if flip else half
-        return (x_high * 4 + y, at_high * 8 + lax.rem(ring + turn, 4) * 2 + core)
-
-    place["to_columns"], place["to_rows"] = to_columns(0, False), to_rows(0, False)
-    place["mask_to"], place["mask_from"] = to_columns(2, True), to_rows(2, True)
+    place["to_columns"] = (to_half * 4 + lax.rem(y + 4 - core, 4), x_low * 8 + z * 2 + core)
+    place["to_rows"] = (x_high * 4 + y, half * 8 + ring * 2 + core)
     place["alone"] = jnp.logical_and(jnp.logical_and(x_low == x_high, z == y), core == 0)
     return place
 
@@ -302,11 +294,9 @@
         copy.start()
     load(0, 0).start()
     load(1, 1).start()
-    for copy in loads[1]:
-        copy.start()
 
     barrier = pltpu.get_barrier_semaphore()
-    peers = [*place["near"], *place["far"], *place["other"], place["mask_from"]]
+    peers = [*place["near"], *place["far"], *place["other"]]
     for peer in peers:
         pl.semaphore_signal(barrier, inc=1, device_id=peer, device_id_type=MESH)
 
@@ -319,7 +309,6 @@
     ring, half = place["ring"], place["half"]
     row_own, col_own = shard_at(mine, y, x_high), shard_at(0, ring, half)
     twin_row, twin_col = shard_at(mine, ring, half), shard_at(0, y, x_high)
-    mask_rows = shard_at(mine, lax.rem(y + 2, 4), 1 - x_high)
     alone = place["alone"]
 
     def first_rows(g):
@@ -485,9 +474,11 @@
 
     moved = [
         ToTwin(copies[0], b_hbm.at[row_own, :], b_own, place["to_columns"], alone),
-        copies[0].to(mask_hbm.at[mask_rows, :], mask_own, place["mask_to"]),
+        ToTwin(copies[0], mask_hbm.at[row_own, :], mask_own, place["to_columns"], alone),
     ]
     first_rows(0)
+    for copy in loads[1]:
+        copy.start()
     multiply_first(0, True)
     reduce_row[0].first()
     first_rows(1)
@@ -507,16 +498,16 @@
     send_other_half(0)
     gather_w0[1].second()
     sums[0].second()
+    w0_moved[1].wait()
+    rows_w0[1].pair()
     rows_w0[0].forward(*rows_w0[0].sent)
     pl.loop(0, 2)(lambda k: multiply_block(0, mine, k))
+    rows_w0[1].first()
     add_other_core(0)
-    w0_moved[1].wait()
-    rows_w0[1].pair()
     gather_w0[1].finish()
     split_columns(cols1, 1)
+    send_other_half(1)
     reduce_col[0].second()
-    rows_w0[1].first()
-    send_other_half(1)
     tile = sums[0].total()
     norm0 = [value_of(tile, g * lines, lines) for g in both]
     curve0 = [value_of(tile, (2 + g) * lines, lines) for g in both]
@@ -531,26 +522,26 @@
     end_second(1)
     make_r2(0)
     sums[2].second()
+    rows_r2[0].first()
+    make_r2(1)
     r2_moved[0].wait()
     gather_r2[0].first()
-    rows_r2[0].first()
-    make_r2(1)
-    gather_r2[0].second()
     rows_r2[0].forward(*rows_r2[0].sent)
-    rows_w0[1].swap(core_peer)
+    rows_r2[1].first()
     r2_moved[1].wait()
     gather_r2[1].first()
-    rows_r2[1].first()
+    gather_r2[0].second()
+    rows_r2[0].swap(core_peer)
+    rows_r2[1].forward(*rows_r2[1].sent)
     gather_r2[0].finish()
-    rows_r2[0].swap(core_peer)
+    gather_r2[1].second()
     split_columns(cols2, 0)
     inner2 = dotted(0, mine)
-    gather_r2[1].second()
-    rows_r2[1].forward(*rows_r2[1].sent)
     rows_r2[0].finish()
+    rows_r2[1].swap(core_peer)
+    rows_w0[1].swap(core_peer)
     sums_of(3, [*shards[0][4:], inner2 + dotted(0, others)])
     gather_r2[1].finish()
-    rows_r2[1].swap(core_peer)
     split_columns(cols2, 1)
     sums[3].second()
     inner2 = dotted(1, mine)

time: 191 us -> 195 us (1.021)
  Pallas kernels: 185 us -> 189 us
    pallas_call x1, Pallas kernels: 185 us -> 189 us  [on_device(): pl.pallas_call(kernel, out_shape=jax.ShapeDtypeStruct((rows, columns), F3...]
where the time goes in v5:
time: 195 us
  Pallas kernels  189 us (97%)
  local copies, waits for them, and re-layouts  5.03 us (3%)
    pallas_call x1, Pallas kernels, on_device(): pl.pallas_call(kernel, out_shape=jax.ShapeDtypeStruct((rows, columns), F3...  189 us
    unnamed x1, local copies, waits for them, and re-layouts  5.03 us

profile of v5, /device:TPU:1, one launch (start us, length us, event | category | flops | bytes accessed | tf_op | source)
XLA Modules:
  0.0 195.1 jit_solution(8389722871331149245)
XLA Ops:
  0.7 189.4 %shard_map.46 = f32[2304,512]{1,0:T(8,128)} custom-call(f32[2304,1152]{1,0:T(8,128)} %h_hbm.1, f32[2304,512]{1,0:T(8,128)} %b_hbm.1, s32[2304,512]{1,0:T(8,128)} %mask_hbm.1, f32[1]{0:T(128)S(6)} %copy.6.damping_ref), custom_call_target="tpu_custom_call" | custom-call | tf_op jit(solution)/shard_map/pallas_call | solution.py:567
  190.1 5.0 %copy.7 = f32[2304,512]{1,0:T(8,128)} copy(f32[2304,512]{1,0:T(8,128)} %shard_map.46) | data formatting | bytes 9437184

commit v6 on v4

--- a/solution.py
+++ b/solution.py
@@ -256,16 +256,8 @@
     place["ring"], place["half"] = ring, half
     to_half = lax.rem(x_high + core, 2)
 
-    def to_columns(turn, flip):
-        at_low = 1 - to_half if flip else to_half
-        return (at_low * 4 + lax.rem(y + 8 - core - turn, 4), x_low * 8 + z * 2 + core)
-
-    def to_rows(turn, flip):
-        at_high = 1 - half if flip else half
-        return (x_high * 4 + y, at_high * 8 + lax.rem(ring + turn, 4) * 2 + core)
-
-    place["to_columns"], place["to_rows"] = to_columns(0, False), to_rows(0, False)
-    place["mask_to"], place["mask_from"] = to_columns(2, True), to_rows(2, True)
+    place["to_columns"] = (to_half * 4 + lax.rem(y + 4 - core, 4), x_low * 8 + z * 2 + core)
+    place["to_rows"] = (x_high * 4 + y, half * 8 + ring * 2 + core)
     place["alone"] = jnp.logical_and(jnp.logical_and(x_low == x_high, z == y), core == 0)
     return place
 
@@ -274,7 +266,7 @@
     h_hbm, b_hbm, mask_hbm, damping_ref, out_hbm,
     h_stage, h_high, h_low, mask, r0, w0_rows, r2_rows, cols1, cols2,
     part0, part1, relay0, got0, relay1, got1, got_core,
-    b_own, mask_own, mask_sent,
+    mask_own, mask_sent,
     v_high, v_low, tile_out, tile_in, stage_sem, in_sem, out_sem, send_sem, receive_sem,
     sums_send, sums_receive,
 ):
@@ -306,7 +298,7 @@
         copy.start()
 
     barrier = pltpu.get_barrier_semaphore()
-    peers = [*place["near"], *place["far"], *place["other"], place["mask_from"]]
+    peers = [*place["near"], *place["far"], *place["other"]]
     for peer in peers:
         pl.semaphore_signal(barrier, inc=1, device_id=peer, device_id_type=MESH)
 
@@ -319,7 +311,6 @@
     ring, half = place["ring"], place["half"]
     row_own, col_own = shard_at(mine, y, x_high), shard_at(0, ring, half)
     twin_row, twin_col = shard_at(mine, ring, half), shard_at(0, y, x_high)
-    mask_rows = shard_at(mine, lax.rem(y + 2, 4), 1 - x_high)
     alone = place["alone"]
 
     def first_rows(g):
@@ -391,14 +382,20 @@
             for copy in moved:
                 copy.wait()
         columns = pl.ds(g * width, width)
-        keep = mask_own[:, columns].astype(F32)
-        r0_here = keep * b_own[:, columns]
-        w0 = keep * (summed + damping * r0_here)
-        cols1[g, col_own, :] = w0
+        cols1[g, col_own, :] = mask_own[:, columns].astype(F32) * summed
         gather_w0[g].first()
         here, there = cols1.at[g, col_own, :], w0_rows.at[g, twin_row, :]
         w0_moved[g] = ToTwin(copies[g], here, there, place["to_rows"], alone)
+
+    def make_w0(g):
+        r0_here = r0[g, row_own, :]
+        return r0_here, w0_rows[g, row_own, :] + damping * r0_here
+
+    def end_move(g):
+        w0_moved[g].wait()
+        r0_here, w0 = make_w0(g)
         dots0[g] = (column_sum(r0_here, r0_here), column_sum(r0_here, w0))
+        rows_w0[g].pair()
 
     def send_other_half(g):
         swaps[g] = []
@@ -427,9 +424,10 @@
 
     def end_second(g):
         summed = reduce_col[g].total()
-        r0_here, w0 = r0[g, row_own, :], w0_rows[g, row_own, :]
+        r0_here, w0 = make_w0(g)
         r1 = r0_here - step0[g] * w0
-        w1 = w0 - step0[g] * (mask_sent[g] * (summed + damping * w0))
+        again = mask_sent[g] * summed + damping * (w0_rows[g, row_own, :] + w0)
+        w1 = w0 - step0[g] * again
         r2_rows[g, row_own, :] = w1
         sums_of(1 + g, [column_sum(r1, r1), column_sum(r1, w1), column_sum(r1, w0)])
 
@@ -439,9 +437,9 @@
         ratio0 = norm1 / (norm0[g] + epsilon)
         curve1 = inner1 + ratio0 * (2.0 * cross1 + ratio0 * curve0[g])
         step1 = norm1 / (curve1 + epsilon)
-        w0 = w0_rows[g, row_own, :]
+        r0_here, w0 = make_w0(g)
         along = r2_rows[g, row_own, :] + ratio0 * w0
-        r2 = (r0[g, row_own, :] - step0[g] * w0) - step1 * along
+        r2 = (r0_here - step0[g] * w0) - step1 * along
         r2_rows[g, row_own, :] = r2
         here, there = r2_rows.at[g, row_own, :], cols2.at[g, twin_col, :]
         r2_moved[g] = ToTwin(copies[g], here, there, place["to_columns"], alone)
@@ -463,8 +461,8 @@
         curve2 = (inner2 + damping * norm2) + ratio1 * (2.0 * cross2 + ratio1 * curve1)
         step2 = norm2 / (curve2 + epsilon)
         on_d1 = step1 + step2 * ratio1
-        on_r0 = step0[g] + on_d1 * (1.0 + ratio0)
         on_w0 = on_d1 * step0[g]
+        on_r0 = step0[g] + on_d1 * (1.0 + ratio0) - on_w0 * damping
 
         @pl.loop(0, 8)
         def _(k):
@@ -484,8 +482,7 @@
         pl.semaphore_wait(barrier, len(peers))
 
     moved = [
-        ToTwin(copies[0], b_hbm.at[row_own, :], b_own, place["to_columns"], alone),
-        copies[0].to(mask_hbm.at[mask_rows, :], mask_own, place["mask_to"]),
+        ToTwin(copies[0], mask_hbm.at[row_own, :], mask_own, place["to_columns"], alone),
     ]
     first_rows(0)
     multiply_first(0, True)
@@ -497,33 +494,31 @@
     end_first(0)
     reduce_row[1].second()
     gather_w0[0].second()
-    w0_moved[0].wait()
-    rows_w0[0].pair()
+    end_move(0)
     end_first(1)
-    sums_of(0, [dots0[0][0], dots0[1][0], dots0[0][1], dots0[1][1]])
     rows_w0[0].first()
     gather_w0[0].finish()
     split_columns(cols1, 0)
     send_other_half(0)
     gather_w0[1].second()
-    sums[0].second()
     rows_w0[0].forward(*rows_w0[0].sent)
     pl.loop(0, 2)(lambda k: multiply_block(0, mine, k))
     add_other_core(0)
-    w0_moved[1].wait()
-    rows_w0[1].pair()
+    end_move(1)
+    sums_of(0, [dots0[0][0], dots0[1][0], dots0[0][1], dots0[1][1]])
     gather_w0[1].finish()
     split_columns(cols1, 1)
     reduce_col[0].second()
+    sums[0].second()
     rows_w0[1].first()
     send_other_half(1)
+    rows_w0[0].swap(core_peer)
+    pl.loop(0, 2)(lambda k: multiply_block(1, mine, k))
+    add_other_core(1)
     tile = sums[0].total()
     norm0 = [value_of(tile, g * lines, lines) for g in both]
     curve0 = [value_of(tile, (2 + g) * lines, lines) for g in both]
     step0 = [norm0[g] / (curve0[g] + epsilon) for g in both]
-    rows_w0[0].swap(core_peer)
-    pl.loop(0, 2)(lambda k: multiply_block(1, mine, k))
-    add_other_core(1)
     rows_w0[1].forward(*rows_w0[1].sent)
     end_second(0)
     reduce_col[1].second()
@@ -586,7 +581,7 @@
             many(ROWS), many(ROWS), many(ROWS), many(WIDTH), many(WIDTH),
             many(WIDTH), many(ROWS),
             many(2, SHARD), many(5, SHARD), many(2, SHARD), many(5, SHARD), many(WIDTH),
-            pltpu.VMEM((SHARD, columns), F32), pltpu.VMEM((SHARD, columns), jnp.int32), many(SHARD),
+            pltpu.VMEM((SHARD, columns), jnp.int32), many(SHARD),
             many(WIDTH, dtype=BF16), many(WIDTH, dtype=BF16),
             pltpu.VMEM((SUMS, 2, 8, 128), F32),
             pltpu.VMEM((SUMS, NEAR + FAR, 8, 128), F32),

time: 191 us -> 176 us (0.921)
  Pallas kernels: 185 us -> 170 us
    pallas_call x1, Pallas kernels: 185 us -> 170 us  [on_device(): pl.pallas_call(kernel, out_shape=jax.ShapeDtypeStruct((rows, columns), F3...]
where the time goes in v6:
time: 176 us
  Pallas kernels  170 us (97%)
  local copies, waits for them, and re-layouts  5.03 us (3%)
    pallas_call x1, Pallas kernels, on_device(): pl.pallas_call(kernel, out_shape=jax.ShapeDtypeStruct((rows, columns), F3...  170 us
    unnamed x1, local copies, waits for them, and re-layouts  5.03 us

profile of v6, /device:TPU:1, one launch (start us, length us, event | category | flops | bytes accessed | tf_op | source)
XLA Modules:
  0.0 176.1 jit_solution(275516977692595422)
XLA Ops:
  0.7 170.4 %shard_map.46 = f32[2304,512]{1,0:T(8,128)} custom-call(f32[2304,1152]{1,0:T(8,128)} %h_hbm.1, f32[2304,512]{1,0:T(8,128)} %b_hbm.1, s32[2304,512]{1,0:T(8,128)} %mask_hbm.1, f32[1]{0:T(128)S(6)} %copy.6.damping_ref), custom_call_target="tpu_custom_call" | custom-call | tf_op jit(solution)/shard_map/pallas_call | solution.py:571
  171.0 5.0 %copy.7 = f32[2304,512]{1,0:T(8,128)} copy(f32[2304,512]{1,0:T(8,128)} %shard_map.46) | data formatting | bytes 9437184

commit v7 on v6

--- a/solution.py
+++ b/solution.py
@@ -131,6 +131,30 @@
         got = self.got
         own = self.part[self.shard(0, False), :]
         return ((own + got[0]) + (got[1] + got[2])) + (got[3] + got[4])
+
+
+class ReduceByAxis(Reduce):
+    def send(self, step, flip, slot):
+        at = self.shard(step, flip)
+        return self.copies.to(self.part.at[at, :], self.got.at[slot], self.device(step, flip and step == 0))
+
+    def first(self):
+        up = self.copies.to(self.part.at[self.shard(2, False), :], self.relay.at[0], self.device(1, False))
+        down = self.copies.to(self.part.at[self.shard(2, True), :], self.relay.at[1], self.device(3, False))
+        self.relays = [up, down]
+        self.sent = [self.send(1, True, 1), self.send(3, False, 2)]
+
+    def third(self):
+        for copy in self.sent:
+            copy.wait()
+        at = self.shard(0, True)
+        self.part[at, :] = self.part[at, :] + (self.got[1] + self.got[3])
+        self.last = self.send(0, True, 4)
+
+    def total(self):
+        own = self.part[self.shard(0, False), :] + (self.got[0] + self.got[2])
+        self.last.wait()
+        return own + self.got[4]
 
 
 class Gather:
@@ -361,10 +385,10 @@
     both = range(groups)
     copies = [Copies(send_sem.at[g], receive_sem.at[g]) for g in both]
     reduce_row = [
-        Reduce(copies[g], part0.at[g], relay0.at[g], got0.at[g], 0, ring, half, place["on_row"]) for g in both
+        ReduceByAxis(copies[g], part0.at[g], relay0.at[g], got0.at[g], 0, ring, half, place["on_row"]) for g in both
     ]
     reduce_col = [
-        Reduce(copies[g], part1.at[g], relay1.at[g], got1.at[g], mine, y, x_high, place["on_col"]) for g in both
+        ReduceByAxis(copies[g], part1.at[g], relay1.at[g], got1.at[g], mine, y, x_high, place["on_col"]) for g in both
     ]
     gather_w0 = [Gather(copies[g], cols1.at[g], 0, ring, half, place["on_row"]) for g in both]
     gather_r2 = [Gather(copies[g], cols2.at[g], 0, ring, half, place["on_row"]) for g in both]
@@ -491,8 +515,10 @@
     multiply_first(1, False)
     reduce_row[0].second()
     reduce_row[1].first()
+    reduce_row[0].third()
+    reduce_row[1].second()
     end_first(0)
-    reduce_row[1].second()
+    reduce_row[1].third()
     gather_w0[0].second()
     end_move(0)
     end_first(1)
@@ -520,8 +546,10 @@
     curve0 = [value_of(tile, (2 + g) * lines, lines) for g in both]
     step0 = [norm0[g] / (curve0[g] + epsilon) for g in both]
     rows_w0[1].forward(*rows_w0[1].sent)
+    reduce_col[0].third()
+    reduce_col[1].second()
     end_second(0)
-    reduce_col[1].second()
+    reduce_col[1].third()
     sums[1].second()
     end_second(1)
     make_r2(0)

time: 176 us -> 173 us (0.983)
  Pallas kernels: 170 us -> 167 us
    pallas_call x1, Pallas kernels: 170 us -> 167 us  [on_device(): pl.pallas_call(kernel, out_shape=jax.ShapeDtypeStruct((rows, columns), F3...]
where the time goes in v7:
time: 173 us
  Pallas kernels  167 us (97%)
  local copies, waits for them, and re-layouts  5.03 us (3%)
    pallas_call x1, Pallas kernels, on_device(): pl.pallas_call(kernel, out_shape=jax.ShapeDtypeStruct((rows, columns), F3...  167 us
    unnamed x1, local copies, waits for them, and re-layouts  5.03 us

profile of v7, /device:TPU:1, one launch (start us, length us, event | category | flops | bytes accessed | tf_op | source)
XLA Modules:
  0.0 172.6 jit_solution(8599247857025152430)
XLA Ops:
  0.7 166.9 %shard_map.46 = f32[2304,512]{1,0:T(8,128)} custom-call(f32[2304,1152]{1,0:T(8,128)} %h_hbm.1, f32[2304,512]{1,0:T(8,128)} %b_hbm.1, s32[2304,512]{1,0:T(8,128)} %mask_hbm.1, f32[1]{0:T(128)S(6)} %copy.6.damping_ref), custom_call_target="tpu_custom_call" | custom-call | tf_op jit(solution)/shard_map/pallas_call | solution.py:599
  167.6 5.0 %copy.7 = f32[2304,512]{1,0:T(8,128)} copy(f32[2304,512]{1,0:T(8,128)} %shard_map.46) | data formatting | bytes 9437184
